TPU v7x, 512 devices: a whole 4x8x8 slice. The times are simulated.
512 devices in a mesh: prow: 16 (over y, core), pcol: 32 (over z, x).
Axes of the slice: x: 4, y: 8, z: 8, core: 2. Of those that a mesh axis runs over, the one named last changes fastest.
Arguments:
- embeddings: bfloat16 [12, 16, 128, 768], P(None, 'prow', None, 'pcol'), may hold values from -6 to 6
- noise_var: bfloat16 [12, 16, 128], P(None, 'prow'), may hold values from 0.5 to 2
Outputs:
- schur_block: float32 [12, 16, 128, 6, 32, 128], P(None, 'prow', None, None, 'pcol')
- panel_cols: float32 [12, 16, 128, 128], P(None, 'prow', 'pcol')
All inputs are finite; a program needn't handle non-finite values.
Results may differ from a plain program's by a relative error of at most 0.0003.
Values may be sent and summed in bfloat16 or wider, within the bound.
A program may use at most 64 MiB of HBM per device.

v0:
```python
import jax
import jax.numpy as jnp
from jax import lax
from jax.sharding import PartitionSpec as P


def from_root(value, axis, source):
    kept = jnp.where(lax.axis_index(axis) == source, value, 0).astype(value.dtype)
    return lax.psum(kept, axis)


def squares(values):
    return jnp.sum(jnp.square(values.astype(jnp.float32)), axis=-1)


def kernel_block(left_x, right_x, left_sq, right_sq, feat_width):
    inner_dots = lax.dot_general(
        left_x, right_x, (((1,), (1,)), ((), ())), preferred_element_type=jnp.float32
    )
    return jnp.exp(-(left_sq[:, None] + right_sq[None, :] - 2.0 * inner_dots) / feat_width)


def shards(embeddings, noise_var):
    row_count = lax.axis_size("prow")
    col_count = lax.axis_size("pcol")
    row_index = lax.axis_index("prow")
    col_index = lax.axis_index("pcol")
    features = lax.all_gather(embeddings, "pcol", axis=3, tiled=True)
    row_tiles = features.shape[0]
    tile_size = features.shape[2]
    feat_width = features.shape[3]
    col_tiles = row_tiles * row_count // col_count
    group_ratio = col_count // row_count
    row_x = features.reshape(row_tiles * tile_size, feat_width)
    row_var = noise_var.reshape(row_tiles * tile_size).astype(jnp.float32)
    first_x, first_noise = (
        from_root(features[0, 0], "prow", 0),
        from_root(noise_var[0, 0], "prow", 0),
    )
    first_var = first_noise.astype(jnp.float32)
    grouped = features.reshape(col_tiles, group_ratio, tile_size, feat_width)
    chosen = lax.dynamic_index_in_dim(grouped, col_index // row_count, 1, keepdims=False)
    root_row = col_index % row_count
    col_x = from_root(chosen, "prow", root_row).reshape(col_tiles * tile_size, feat_width)
    row_sq = squares(row_x)
    col_sq = squares(col_x)
    first_sq = squares(first_x)
    offsets = jnp.arange(tile_size, dtype=jnp.int32)
    row_global = (
        (jnp.arange(row_tiles, dtype=jnp.int32) * row_count + row_index)[:, None] * tile_size
        + offsets[None, :]
    ).reshape(-1)
    col_global = (
        (jnp.arange(col_tiles, dtype=jnp.int32) * col_count + col_index)[:, None] * tile_size
        + offsets[None, :]
    ).reshape(-1)
    kernel_local = kernel_block(row_x, col_x, row_sq, col_sq, feat_width)
    kernel_local = kernel_local + jnp.where(
        row_global[:, None] == col_global[None, :], row_var[:, None], jnp.float32(0.0)
    )
    first_kernel = kernel_block(first_x, first_x, first_sq, first_sq, feat_width)
    first_kernel = first_kernel + jnp.where(
        offsets[:, None] == offsets[None, :], first_var[None, :], jnp.float32(0.0)
    )
    factor = jnp.linalg.cholesky(first_kernel)
    candidate = lax.linalg.triangular_solve(
        factor, kernel_local[:, :tile_size], left_side=False, lower=True, transpose_a=True
    )
    row_panel = from_root(candidate, "pcol", 0)
    regrouped = row_panel.reshape(col_tiles, group_ratio, tile_size, tile_size)
    picked = lax.dynamic_index_in_dim(regrouped, col_index // row_count, 1, keepdims=False)
    col_panel = from_root(picked, "prow", root_row).reshape(col_tiles * tile_size, tile_size)
    update = lax.dot_general(
        row_panel,
        col_panel,
        (((1,), (1,)), ((), ())),
        precision=lax.Precision.HIGHEST,
        preferred_element_type=jnp.float32,
    )
    schur_block = (kernel_local - update).reshape(row_tiles, 1, tile_size, col_tiles, 1, tile_size)
    share = tile_size // col_count
    panel_cols = lax.dynamic_slice_in_dim(
        row_panel.reshape(row_tiles, 1, tile_size, tile_size), col_index * share, share, 2
    )
    return (schur_block, panel_cols)


def solution(mesh):
    placed = (P(None, "prow", None, "pcol"), P(None, "prow", None))
    return jax.shard_map(
        shards,
        mesh=mesh,
        in_specs=placed,
        out_specs=(P(None, "prow", None, None, "pcol", None), P(None, "prow", "pcol", None)),
        check_vma=False,
    )
```

profile of v0, /device:TPU:1, one launch (start us, length us, event | category | flops | bytes accessed | tf_op | source)
XLA Modules:
  0.0 566.9 jit_solution(10739975928645798636)
XLA Ops:
  7.2 0.0 copy-start.2
  7.2 0.0 all-gather.2.cloned.1.call-start
  7.2 0.7 all-gather.2.cloned.1.call-update
  7.9 0.0 all-reduce.9.cloned.1.call-start
  8.0 0.7 fusion.9
  8.7 29.8 %psum.37 = bf16[128]{0:T(256)(128)(2,1)S(1)} all-reduce(bf16[128]{0:T(256)(128)(2,1)S(1)} %fusion.9), channel_id=1, replica_groups=mesh['prow'=16,'pcol'=32] {'prow'}, use_global_device_ids=true, to_apply=%region_5.6 | all-reduce | flops 128 | bytes 512 | tf_op jit(solution)/shard_map/psum | solution.py:9
  38.5 0.1 add_bitcast_fusion
  38.6 57.0 %all-gather.2.cloned.1.call-done = bf16[12,1,128,768]{2,3,1,0:T(8,128)(2,1)} async-done(((bf16[12,1,128,24]{2,3,1,0:T(8,128)(2,1)}), bf16[12,1,128,768]{2,3,1,0:T(8,128)(2,1)}) %all-gather.2.cloned.1.call-update) | async-done | bytes 2359312 | tf_op jit(solution)/shard_map/all_gather | solution.py:28
  95.6 0.0 copy-start
  95.6 4.4 copy.23
  100.0 2.4 select_bitcast_fusion
  102.4 0.0 copy-done
  102.4 0.7 fusion.5
  103.1 0.0 all-reduce.9.cloned.1.call-update
  103.1 0.0 all-reduce.5.cloned.1.call-start
  103.2 0.1 add_bitcast_fusion.1
  103.2 0.0 copy-done.2
  103.2 0.5 multiply_reduce_fusion
  103.7 119.9 %all-reduce.9.cloned.1.call-done = (bf16[6,128,768]{2,1,0:T(8,128)(2,1)}, bf16[128,768]{0,1:T(8,128)(2,1)}) async-done(((bf16[6,128,768]{2,1,0:T(8,128)(2,1)}, bf16[128,768]{0,1:T(8,128)(2,1)}), (bf16[6,128,768]{2,1,0:T(8,128)(2,1)}, bf16[128,768]{0,1:T(8,128)(2,1)})) %all-reduce.9.cloned.1.call-update) | async-done | bytes 1376272 | tf_op jit(solution)/shard_map/psum | solution.py:9
  223.6 1.0 multiply_reduce_fusion.2
  224.6 1.3 broadcast_add_fusion
  225.9 0.1 copy.25
  226.0 1.6 multiply_reduce_fusion.1
  227.6 0.1 copy.26
  227.7 0.1 add_multiply_fusion
  227.8 11.7 %cholesky.16 = f32[128,128]{1,0:T(8,128)S(1)} custom-call(f32[128,128]{1,0:T(8,128)S(1)} %add_multiply_fusion), custom_call_target="Cholesky" | custom-call | tf_op jit(solution)/shard_map/jit(cholesky)/cholesky | solution.py:65
  239.5 0.6 compare_reduce_fusion
  240.2 0.7 fusion.6
  240.8 9.8 %custom-call.6 = f32[1,128,128]{1,2,0:T(8,128)S(1)} custom-call(f32[1,128,128]{2,1,0:T(8,128)S(1)} %fusion.6), custom_call_target="InvertDiagBlocksLowerTriangular" | custom-call | tf_op jit(solution)/shard_map/triangular_solve | solution.py:66
  250.6 4.6 fusion.3
  255.3 0.0 copy-start.1
  255.3 2.2 copy-done.1
  257.4 2.3 convolution_select_fusion
  259.8 0.0 all-reduce.5.cloned.1.call-update
  259.8 0.2 all-reduce.7.cloned.1.call-start
  260.0 156.8 %all-reduce.5.cloned.1.call-done = f32[1536,128]{1,0:T(8,128)} async-done(((f32[1536,128]{1,0:T(8,128)}), f32[1536,128]{1,0:T(8,128)}) %all-reduce.5.cloned.1.call-update) | async-done | bytes 786448 | tf_op jit(solution)/shard_map/psum | solution.py:9
  416.8 1.8 dynamic-slice_select_fusion
  418.6 0.0 all-reduce.7.cloned.1.call-update
  418.6 1.4 constant_dynamic-slice_fusion
  420.0 115.0 %all-reduce.7.cloned.1.call-done = f32[768,128]{1,0:T(8,128)} async-done(((f32[768,128]{1,0:T(8,128)}), f32[768,128]{1,0:T(8,128)}) %all-reduce.7.cloned.1.call-update) | async-done | bytes 393232 | tf_op jit(solution)/shard_map/psum | solution.py:9
  535.0 8.7 %convolution_subtract_fusion = f32[1536,768]{0,1:T(8,128)} fusion(f32[1536,768]{0,1:T(8,128)} %copy-done.1, f32[1536,128]{1,0:T(8,128)} %all-reduce.5.cloned.1.call-done, f32[768,128]{1,0:T(8,128)} %all-reduce.7.cloned.1.call-done), kind=kOutput, calls=%fused_computation.6 | convolution fusion | flops 1813118976 | bytes 10616832 | tf_op jit(solution)/shard_map/dot_general | solution.py:73
  543.8 6.7 %reshape.116 = f32[12,1,128,6,1,128]{2,0,5,3,4,1:T(8,128)} reshape(f32[1536,768]{0,1:T(8,128)} %convolution_subtract_fusion) | data formatting | bytes 9437184 | tf_op jit(solution)/shard_map/reshape | solution.py:80
  550.4 9.9 %copy.30 = f32[12,1,128,6,1,128]{5,4,3,2,1,0:T(1,128)} copy(f32[12,1,128,6,1,128]{2,0,5,3,4,1:T(8,128)} %reshape.116) | data formatting | bytes 9437184
  (5 shorter events, 0.1 us)
Async XLA Ops:
  7.2 96.1 %copy-start.2 = (bf16[12,1,128]{2,0,1:T(8,128)(2,1)S(1)}, bf16[12,1,128]{2,0,1:T(8,128)(2,1)}, u32[]{:S(2)}) copy-start(bf16[12,1,128]{2,0,1:T(8,128)(2,1)} %param.3) | copy-start | bytes 9220
  7.2 88.4 %all-gather.2.cloned.1.call-start = ((), (), s32[]{:S(2)}) async-start(), calls=%async_computation | async-start | bytes 2433024 | tf_op jit(solution)/shard_map/all_gather | solution.py:28
  7.9 215.7 %all-reduce.9.cloned.1.call-start = ((), (), s32[]{:S(2)}) async-start(), calls=%async_computation.3 | async-start | bytes 2752512 | tf_op jit(solution)/shard_map/psum | solution.py:9
  95.6 6.8 %copy-start = (bf16[12,1,128,768]{2,3,1,0:T(8,128)(2,1)S(1)}, bf16[12,1,128,768]{2,3,1,0:T(8,128)(2,1)}, u32[]{:S(2)}) copy-start(bf16[12,1,128,768]{2,3,1,0:T(8,128)(2,1)} %all-gather.2.cloned.1.call-done) | copy-start | bytes 7077892
  103.1 313.7 %all-reduce.5.cloned.1.call-start = ((), (), s32[]{:S(2)}) async-start(), calls=%async_computation.1 | async-start | bytes 1572864 | tf_op jit(solution)/shard_map/psum | solution.py:9
  255.3 2.2 copy-start.1
  259.8 275.2 %all-reduce.7.cloned.1.call-start = ((), (), s32[]{:S(2)}) async-start(), calls=%async_computation.2 | async-start | bytes 786432 | tf_op jit(solution)/shard_map/psum | solution.py:9
Sparse Core Ops, SparseCore 0:
  11.1 84.4 all-gather.1
  103.2 120.3 all-reduce.8
  259.9 156.8 all-reduce.4
  418.9 116.0 all-reduce.6
where the time goes:
time: 568 us; the launch traced here: 567 us
  waiting for transfers between devices  449 us (79%)
  other arithmetic  31.8 us (6%)
  blocking collectives  29.8 us (5%)
  local copies, waits for them, and re-layouts  24.8 us (4%)
  matrix products  16.9 us (3%)
  between operations  13.9 us (2%)
    psum x3, waiting for transfers between devices, from_root(): return lax.psum(kept, axis)  392 us
    all_gather x1, waiting for transfers between devices, shards(): features = lax.all_gather(embeddings, 'pcol', axis=3, tiled=True)  57 us
    psum x1, blocking collectives, from_root(): return lax.psum(kept, axis)  29.8 us
    another operation x3, other arithmetic, shards(): factor = jnp.linalg.cholesky(first_kernel)  12.4 us
    unnamed x7, local copies, waits for them, and re-layouts  12.1 us
  transfers between devices with their start and end apart: 4, of which 4 were waited for; matrix products, arithmetic and copies ran while one was open for 0% of the time, Pallas kernels for 0%

commit v1 on v0

v1 whole, which is shorter than its diff:
```python
import functools

import jax
import jax.numpy as jnp
from jax import lax
from jax.experimental import pallas as pl
from jax.experimental.pallas import tpu as pltpu
from jax.sharding import PartitionSpec as P

F32 = jnp.float32
BF16 = jnp.bfloat16


def from_root(value, axis, source):
    kept = jnp.where(lax.axis_index(axis) == source, value, 0).astype(value.dtype)
    return lax.psum(kept, axis)


def feature_squares(block):
    wide = block.astype(F32)
    return jnp.sum(wide * wide, axis=0, keepdims=True)


def down(row):
    tile = row.shape[1]
    return jnp.transpose(jnp.broadcast_to(row, (tile, tile)))


def eye_mask(tile):
    rows = lax.broadcasted_iota(jnp.int32, (tile, tile), 0)
    cols = lax.broadcasted_iota(jnp.int32, (tile, tile), 1)
    return rows == cols


def split3(panel, left):
    high = panel.astype(BF16)
    low = (panel - high.astype(F32)).astype(BF16)
    return jnp.concatenate([high, high, low] if left else [high, low, high], axis=1)


def matmul(left, right):
    return lax.dot_general(left, right, (((1,), (0,)), ((), ())), preferred_element_type=F32)


def matmul_nt(left, right, precision=None):
    return lax.dot_general(
        left, right, (((1,), (1,)), ((), ())), precision=precision, preferred_element_type=F32
    )


def inverse_factor(first, noise, work):
    feats, tile = first.shape
    sq = feature_squares(first)
    dots = matmul(jnp.transpose(first), first)
    gram = jnp.exp((2.0 * dots - (down(sq) + sq)) * (1.0 / feats))
    diagonal = eye_mask(tile)
    work[...] = gram + jnp.where(diagonal, noise, 0.0)
    part = tile // 4
    for base in range(0, tile, part):
        height = tile - base
        lanes = lax.broadcasted_iota(jnp.int32, (height, tile), 1)
        ids = lax.broadcasted_iota(jnp.int32, (height, tile), 0) + base

        def step(k, carry, base=base, lanes=lanes, ids=ids):
            held = work[base:, :]
            at_k = lanes == k
            pivot = work[pl.ds(k, 1), :]
            here = at_k[:1]
            inv = 1.0 / jnp.sum(jnp.where(here, pivot, 0.0), axis=1, keepdims=True)
            column = jnp.sum(jnp.where(at_k, held, 0.0), axis=1, keepdims=True)
            scaled = jnp.where(here, 1.0, pivot) * inv
            factor = jnp.where(ids > k, column, 0.0)
            cleared = jnp.where(at_k & (ids > k), 0.0, held)
            work[base:, :] = cleared - factor * scaled
            return carry

        lax.fori_loop(base, base + part, step, 0)
    done = work[...]
    pivots = jnp.sum(jnp.where(diagonal, done, 0.0), axis=1, keepdims=True)
    rows = lax.broadcasted_iota(jnp.int32, (tile, tile), 0)
    cols = lax.broadcasted_iota(jnp.int32, (tile, tile), 1)
    unit = jnp.where(cols < rows, done, jnp.where(diagonal, 1.0, 0.0))
    return unit * (1.0 / jnp.sqrt(pivots))


def factor_kernel(first_ref, noise_ref, inverse_ref, work):
    inverse_ref[...] = inverse_factor(first_ref[...], noise_ref[...], work)


def schur_kernel(
    row_count, col_count, row_ref, col_ref, first_ref, noise_ref, inverse_ref,
    schur_ref, share_ref, wide, col_sq, col_panel, panel,
):
    step = pl.program_id(0)
    group, feats, tile = row_ref.shape
    col_tiles = col_ref.shape[0]
    scale = 1.0 / feats
    r, q = lax.axis_index("prow"), lax.axis_index("pcol")
    diagonal = eye_mask(tile)
    first = first_ref[...]
    first_sq = feature_squares(first)
    inverse = inverse_ref[...]

    def panel_of(samples, sq, noise, is_first):
        gram = jnp.exp((2.0 * matmul(samples, first) - (sq + first_sq)) * scale)
        gram = gram + jnp.where(diagonal & is_first, noise, 0.0)
        return matmul_nt(gram, inverse, lax.Precision.HIGHEST)

    @pl.when(step == 0)
    def _():
        for d in range(col_tiles):
            block = col_ref[d]
            place = slice(d * tile, (d + 1) * tile)
            wide[:, place] = block
            sq = feature_squares(block)
            col_sq[:, place] = sq
            noise = noise_ref[noise_ref.shape[0] - 1 :, :]
            is_first = (q == 0) if d == 0 else False
            col_panel[place, :] = split3(
                panel_of(jnp.transpose(block), down(sq), noise, is_first), False
            )

    stride = col_tiles
    share = tile // col_count
    shares = []
    for t in range(group):
        a = step * group + t
        block = row_ref[t]
        samples = jnp.transpose(block)
        sq = down(feature_squares(block))
        noise = noise_ref[pl.ds(a, 1), :]
        rows = panel_of(samples, sq, noise, a * row_count + r == 0)
        panel[t * tile : (t + 1) * tile, :] = rows
        dots = matmul(samples, wide[...])
        update = matmul_nt(split3(rows, True), col_panel[...])
        for d in range(col_tiles):
            place = slice(d * tile, (d + 1) * tile)
            gram = jnp.exp((2.0 * dots[:, place] - (sq + col_sq[:, place])) * scale)
            same = a * row_count + r == d * col_count + q
            gram = gram + jnp.where(diagonal & same, noise, 0.0)
            schur_ref[pl.ds(t * tile * stride + d, tile, stride=stride), :] = gram - update[:, place]
        shares.append(panel[pl.ds(t * tile + q * share, share), :])
    share_ref[...] = jnp.concatenate(shares, axis=0)


def shards(embeddings, noise_var):
    row_count, col_count = lax.axis_size("prow"), lax.axis_size("pcol")
    col_index = lax.axis_index("pcol")
    local = jnp.transpose(embeddings[:, 0], (0, 2, 1))
    rows = lax.all_gather(local, "pcol", axis=1, tiled=True)
    row_tiles, feats, tile = rows.shape
    col_tiles = row_tiles * row_count // col_count
    ratio = col_count // row_count
    first, first_noise = from_root(rows[0], "prow", 0), from_root(noise_var[0, 0], "prow", 0)
    chosen = lax.dynamic_index_in_dim(
        rows.reshape(col_tiles, ratio, feats, tile), col_index // row_count, 1, keepdims=False
    )
    cols = from_root(chosen, "prow", col_index % row_count)
    return finish(rows, cols, first, noise_var, first_noise)


def finish(rows, cols, first, noise_var, first_noise):
    row_count, col_count = lax.axis_size("prow"), lax.axis_size("pcol")
    row_tiles, feats, tile = rows.shape
    col_tiles = cols.shape[0]
    noise = jnp.concatenate([noise_var[:, 0], first_noise[None]], axis=0).astype(F32)
    inverse = pl.pallas_call(
        factor_kernel,
        out_shape=jax.ShapeDtypeStruct((tile, tile), F32),
        scratch_shapes=[pltpu.VMEM((tile, tile), F32)],
        name="factor",
    )(first, noise[row_tiles:])
    group = 2
    share = tile // col_count
    height = group * tile * col_tiles
    schur, shared = pl.pallas_call(
        functools.partial(schur_kernel, row_count, col_count),
        grid=(row_tiles // group,),
        in_specs=[
            pl.BlockSpec((group, feats, tile), lambda i: (i, 0, 0)),
            pl.BlockSpec((col_tiles, feats, tile), lambda i: (0, 0, 0)),
            pl.BlockSpec((feats, tile), lambda i: (0, 0)),
            pl.BlockSpec((row_tiles + 1, tile), lambda i: (0, 0)),
            pl.BlockSpec((tile, tile), lambda i: (0, 0)),
        ],
        out_specs=[
            pl.BlockSpec((height, tile), lambda i: (i, 0)),
            pl.BlockSpec((group * share, tile), lambda i: (i, 0)),
        ],
        out_shape=[
            jax.ShapeDtypeStruct((row_tiles * tile * col_tiles, tile), F32),
            jax.ShapeDtypeStruct((row_tiles * share, tile), F32),
        ],
        scratch_shapes=[
            pltpu.VMEM((feats, col_tiles * tile), BF16),
            pltpu.VMEM((1, col_tiles * tile), F32),
            pltpu.VMEM((col_tiles * tile, 3 * tile), BF16),
            pltpu.VMEM((group * tile, tile), F32),
        ],
        name="schur",
    )(rows, cols, first, noise, inverse)
    return (
        schur.reshape(row_tiles, 1, tile, col_tiles, 1, tile),
        shared.reshape(row_tiles, 1, share, tile),
    )


def solution(mesh):
    placed = (P(None, "prow", None, "pcol"), P(None, "prow", None))
    return jax.shard_map(
        shards,
        mesh=mesh,
        in_specs=placed,
        out_specs=(P(None, "prow", None, None, "pcol", None), P(None, "prow", "pcol", None)),
        check_vma=False,
    )
```

time: 568 us -> 254 us (0.45)
  waiting for transfers between devices: 449 us -> 182 us
  other arithmetic: 31.8 us -> 4 us
  Pallas kernels: 0 us -> 27.2 us
  local copies, waits for them, and re-layouts: 24.8 us -> 0.52 us
  matrix products: 16.9 us -> 0 us
    psum x3 -> x1, waiting for transfers between devices: 392 us -> 93.3 us  [from_root(): return lax.psum(kept, axis)]
    all_gather x1, waiting for transfers between devices: 57 us -> 87.5 us  [shards(): rows = lax.all_gather(local, 'pcol', axis=1, tiled=True)]
    pallas_call x0 -> x2, Pallas kernels: none -> 27.2 us  [the longest x1 14 us: finish(): pl.pallas_call(factor_kernel, out_shape=jax.ShapeDtypeStruct((tile, tile)...]
    another operation x5 -> x0, other arithmetic: 22.9 us -> none  [the longest x3 12.4 us: shards(): factor = jnp.linalg.cholesky(first_kernel)]
    dot_general x3 -> x0, matrix products: 14.6 us -> none  [the longest x1 8.75 us: shards(): lax.dot_general(row_panel, col_panel, (((1,), (1,)), ((), ())), precision...]
    unnamed x7 -> x4, local copies, waits for them, and re-layouts: 12.1 us -> 0.01 us
    reshape x1 -> x0, local copies, waits for them, and re-layouts: 6.68 us -> none  [shards(): (kernel_local - update).reshape(row_tiles, 1, tile_size, col_tiles, 1, ti...]
  transfers between devices with their start and end apart: 4 -> 2, of which waited for: 4 -> 2; matrix products, arithmetic and copies ran while one was open for 0% -> 0% of each run, Pallas kernels for 0% -> 0%
where the time goes in v1:
time: 254 us
  waiting for transfers between devices  182 us (72%)
  Pallas kernels  27.2 us (11%)
  blocking collectives  26.7 us (11%)
  between operations  14.1 us (6%)
  other arithmetic  4 us (2%)
    psum x1, waiting for transfers between devices, from_root(): return lax.psum(kept, axis)  93.3 us
    all_gather x1, waiting for transfers between devices, shards(): rows = lax.all_gather(local, 'pcol', axis=1, tiled=True)  87.5 us
    psum x1, blocking collectives, from_root(): return lax.psum(kept, axis)  26.7 us
    pallas_call x1, Pallas kernels, finish(): pl.pallas_call(factor_kernel, out_shape=jax.ShapeDtypeStruct((tile, tile)...  14 us
    pallas_call x1, Pallas kernels, finish(): pl.pallas_call(functools.partial(schur_kernel, row_count, col_count), gri...  13.2 us
  transfers between devices with their start and end apart: 2, of which 2 were waited for; matrix products, arithmetic and copies ran while one was open for 0% of the time, Pallas kernels for 0%

profile of v1, /device:TPU:1, one launch (start us, length us, event | category | flops | bytes accessed | tf_op | source)
XLA Modules:
  0.0 254.1 jit_solution(10460586446551486860)
XLA Ops:
  7.2 0.0 all-gather.2.cloned.1.call-start
  7.2 0.7 all-gather.2.cloned.1.call-update
  7.9 0.0 all-reduce.3.cloned.1.call-start
  8.0 87.5 %all-gather.2.cloned.1.call-done.row_ref = bf16[12,768,128]{2,1,0:T(8,128)(2,1)} async-done(((bf16[12,24,128]{2,1,0:T(8,128)(2,1)}), bf16[12,768,128]{2,1,0:T(8,128)(2,1)}) %all-gather.2.cloned.1.call-update) | async-done | bytes 2359312 | tf_op jit(solution)/shard_map/all_gather | solution.py:150
  95.4 2.4 fusion
  97.8 0.0 copy-start.1
  97.8 1.6 fusion.1
  99.4 0.0 all-reduce.3.cloned.1.call-update
  99.4 0.0 copy-done.1
  99.5 26.7 %psum.23 = bf16[1,128]{1,0:T(2,128)(2,1)S(1)} all-reduce(bf16[1,128]{1,0:T(2,128)(2,1)S(1)} %fusion.2), channel_id=1, replica_groups=mesh['prow'=16,'pcol'=32] {'prow'}, use_global_device_ids=true, to_apply=%region_2.3 | all-reduce | flops 128 | bytes 512 | tf_op jit(solution)/shard_map/psum | solution.py:16
  126.1 0.0 copy-start
  126.1 0.5 slice.13.noise_ref
  126.7 93.3 %all-reduce.3.cloned.1.call-done = (bf16[6,768,128]{2,1,0:T(8,128)(2,1)}, bf16[768,128]{1,0:T(8,128)(2,1)}) async-done(((bf16[6,768,128]{2,1,0:T(8,128)(2,1)}, bf16[768,128]{1,0:T(8,128)(2,1)}), (bf16[6,768,128]{2,1,0:T(8,128)(2,1)}, bf16[768,128]{1,0:T(8,128)(2,1)})) %all-reduce.3.cloned.1.call-update) | async-done | bytes 1376272 | tf_op jit(solution)/shard_map/psum | solution.py:16
  220.0 14.0 %factor.1.inverse_ref = f32[128,128]{1,0:T(8,128)} custom-call(bf16[768,128]{1,0:T(8,128)(2,1)} %get-tuple-element.11.first_ref, f32[1,128]{1,0:T(1,128)} %slice.13.noise_ref), custom_call_target="tpu_custom_call" | custom-call | tf_op jit(solution)/shard_map/factor/pallas_call | solution.py:167
  234.1 0.0 copy-done
  234.1 13.2 %schur.1 = (f32[9216,128]{1,0:T(8,128)}, f32[48,128]{1,0:T(8,128)}) custom-call(bf16[12,768,128]{2,1,0:T(8,128)(2,1)} %all-gather.2.cloned.1.call-done.row_ref, bf16[6,768,128]{2,1,0:T(8,128)(2,1)} %get-tuple-element.10.col_ref, bf16[768,128]{1,0:T(8,128)(2,1)} %get-tuple-element.11.first_ref, f32[13,128]{1,0:T(8,128)} %copy-done, f32[128,128]{1,0:T(8,128)} %factor.1.inverse_ref), custom_call_target="tpu_custom_call" | custom-call | tf_op jit(solution)/shard_map/schur/pallas_call | solution.py:176
  (2 shorter events, 0.0 us)
Async XLA Ops:
  7.2 88.3 %all-gather.2.cloned.1.call-start = ((), (), s32[]{:S(2)}) async-start(), calls=%async_computation | async-start | bytes 2433024 | tf_op jit(solution)/shard_map/all_gather | solution.py:150
  7.9 212.1 %all-reduce.3.cloned.1.call-start = ((), (), s32[]{:S(2)}) async-start(), calls=%async_computation.1 | async-start | bytes 2752512 | tf_op jit(solution)/shard_map/psum | solution.py:16
  97.8 1.6 copy-start.1
  126.1 107.9 %copy-start = (f32[13,128]{1,0:T(8,128)}, f32[13,128]{1,0:T(8,128)S(1)}, u32[]{:S(2)}) copy-start(f32[13,128]{1,0:T(8,128)S(1)} %maximum_convert_fusion.noise_ref) | copy-start | bytes 19972
Sparse Core Ops, SparseCore 0:
  11.1 84.2 all-gather.1
  99.6 120.3 all-reduce.2

commit v2 on v1

--- a/solution.py
+++ b/solution.py
@@ -9,11 +9,6 @@
 
 F32 = jnp.float32
 BF16 = jnp.bfloat16
-
-
-def from_root(value, axis, source):
-    kept = jnp.where(lax.axis_index(axis) == source, value, 0).astype(value.dtype)
-    return lax.psum(kept, axis)
 
 
 def feature_squares(block):
@@ -143,20 +138,289 @@
     share_ref[...] = jnp.concatenate(shares, axis=0)
 
 
+def gather_kernel(
+    shape, local, noise, rows, cols, first, first_noise,
+    held, own_sem, lead_send, lead_recv, x_send, x_recv, z_send, z_recv, y_send, y_recv, root_sem,
+):
+    nx, nz, ny = shape
+    col_tiles, ratio = rows.shape[:2]
+    half = col_tiles // 2
+    r, q = lax.axis_index("prow"), lax.axis_index("pcol")
+    x, z = lax.rem(q, nx), lax.div(q, nx)
+    core, y = lax.rem(r, 2), lax.div(r, 2)
+    prow, total = 2 * ny, nx * nz
+    owner = lax.rem(q, prow)
+    side = lax.div(q, prow)
+    place = lax.rem(y - lax.div(owner, 2) + ny, ny)
+    on_line = core == lax.rem(owner, 2)
+    is_root = on_line & (place == 0)
+    is_relay = on_line & (place != 0)
+    is_lead = r == 0
+    far = ny // 2
+    goes_up = place < far
+    goes_down = (place == 0) | (place > far + 1)
+
+    def near_z(shift):
+        return lax.rem(z + shift + nz, nz)
+
+    def x_peer(k):
+        return nx * z + lax.rem(x + k, nx)
+
+    def z_peer(shift):
+        return nx * near_z(shift) + x
+
+    def y_peer(shift):
+        return 2 * lax.rem(y + shift + ny, ny) + core
+
+    def remote(src, dst, send, recv, row, col):
+        return pltpu.make_async_remote_copy(
+            src_ref=src, dst_ref=dst, send_sem=send, recv_sem=recv,
+            device_id=(row, col), device_id_type=pl.DeviceIdType.MESH,
+        )
+
+    barrier = pltpu.get_barrier_semaphore()
+    for k in range(1, prow):
+        pl.semaphore_signal(
+            barrier, device_id=(lax.rem(r + k, prow), q), device_id_type=pl.DeviceIdType.MESH
+        )
+    peers = [x_peer(k) for k in range(1, nx)] + [z_peer(1), z_peer(-1)]
+    for peer in peers:
+        pl.semaphore_signal(barrier, device_id=(r, peer), device_id_type=pl.DeviceIdType.MESH)
+    pl.semaphore_wait(barrier, prow - 1 + len(peers))
+
+    def lead(k):
+        return [
+            remote(local.at[0, 0], first.at[z, x], lead_send.at[0, k - 1], lead_recv.at[0], k, q),
+            remote(noise, first_noise, lead_send.at[1, k - 1], lead_recv.at[1], k, q),
+        ]
+
+    own_lead = [
+        pltpu.make_async_copy(local.at[0, 0], first.at[z, x], own_sem.at[1]),
+        pltpu.make_async_copy(noise, first_noise, own_sem.at[2]),
+    ]
+
+    @pl.when(is_lead)
+    def _():
+        for k in range(1, prow):
+            for copy in lead(k):
+                copy.start()
+        for copy in own_lead:
+            copy.start()
+
+    own = pltpu.make_async_copy(local, rows.at[:, :, z, x], own_sem.at[0])
+    own.start()
+
+    def part(chunk, at_z, at_x=None):
+        spot = (at_z,) if at_x is None else (at_z, at_x)
+        if chunk == 0:
+            return first.at[spot]
+        tiles = pl.ds((chunk - 1) * half, half)
+        return rows.at[(tiles, slice(None), *spot)]
+
+    def x_copy(chunk, k):
+        source = part(0, z, x) if chunk == 0 else local.at[pl.ds((chunk - 1) * half, half)]
+        return remote(
+            source, part(chunk, z, x), x_send.at[chunk, k - 1], x_recv.at[chunk, k - 1], r, x_peer(k)
+        )
+
+    for chunk in (1, 2):
+        for k in range(1, nx):
+            x_copy(chunk, k).start()
+
+    @pl.when(is_lead)
+    def _():
+        for copy in own_lead:
+            copy.wait()
+
+    @pl.when(jnp.logical_not(is_lead))
+    def _():
+        for copy in lead(1):
+            copy.wait_recv()
+
+    for k in range(1, nx):
+        x_copy(0, k).start()
+
+    last = nz // 2
+
+    def has(way, step, chunk):
+        return step < last or (chunk == 2) == (way == 1)
+
+    def z_send_copy(way, step, chunk):
+        toward = 1 if way == 0 else -1
+        block = part(chunk, near_z(-toward * (step - 1)))
+        return remote(
+            block, block, z_send.at[way, step - 1, chunk], z_recv.at[way, step - 1, chunk],
+            r, z_peer(toward),
+        )
+
+    def z_arrived(way, step, chunk):
+        toward = 1 if way == 0 else -1
+        block = part(chunk, near_z(-toward * step))
+        remote(
+            block, block, z_send.at[way, step - 1, chunk], z_recv.at[way, step - 1, chunk],
+            r, z_peer(toward),
+        ).wait_recv()
+
+    def y_group(step):
+        ways = (0,) if step == 0 else (0, 1)
+        return [
+            (step, way, piece) for piece in (0, 1) for way in ways
+            if step == 0 or has(way, step, piece + 1)
+        ]
+
+    y_order = [item for step in range(last + 1) for item in y_group(step)]
+
+    def y_place(item):
+        step, way, _ = item
+        return near_z(-step if way == 0 else step)
+
+    def col_part(item):
+        return cols.at[pl.ds(item[2] * half, half), y_place(item)]
+
+    def y_copies(item, from_rows):
+        i = y_order.index(item)
+        tiles = pl.ds(item[2] * half, half)
+        source = rows.at[tiles, side, y_place(item)] if from_rows else col_part(item)
+        to = [y_peer(1), y_peer(-1), 2 * y + 1 - core]
+        return [
+            remote(source, col_part(item), y_send.at[i, n], y_recv.at[i], row, q)
+            for n, row in enumerate(to)
+        ]
+
+    def each_way(copies, act):
+        pl.when(goes_up)(lambda: act(copies[0]))
+        pl.when(goes_down)(lambda: act(copies[1]))
+        act(copies[2])
+
+    def keep(item):
+        i = y_order.index(item)
+        tiles = pl.ds(item[2] * half, half)
+        buffer = held.at[tiles, y_place(item)]
+        return (
+            pltpu.make_async_copy(rows.at[tiles, side, y_place(item)], buffer, root_sem.at[0, i]),
+            pltpu.make_async_copy(buffer, col_part(item), root_sem.at[1, i]),
+        )
+
+    def y_start(item):
+        @pl.when(is_root)
+        def _():
+            each_way(y_copies(item, True), lambda copy: copy.start())
+            keep(item)[0].start()
+
+    def y_relay(item):
+        @pl.when(is_relay)
+        def _():
+            copies = y_copies(item, False)
+            copies[2].wait_recv()
+            each_way(copies, lambda copy: copy.start())
+
+    for chunk in (0, 1, 2):
+        if chunk == 1:
+            own.wait()
+        for k in range(1, nx):
+            x_copy(chunk, k).wait_recv()
+        for way in (0, 1):
+            z_send_copy(way, 1, chunk).start()
+        if chunk:
+            y_start((0, 0, chunk - 1))
+    lag = 2
+    for step in range(2, last + 2):
+        for chunk in (0, 1, 2):
+            for way in (0, 1):
+                if has(way, step - 1, chunk):
+                    z_arrived(way, step - 1, chunk)
+                    if step <= last and has(way, step, chunk):
+                        z_send_copy(way, step, chunk).start()
+                    if chunk:
+                        y_start((step - 1, way, chunk - 1))
+        if step - 1 >= lag:
+            for item in y_group(step - 1 - lag):
+                y_relay(item)
+    for step in range(last + 1 - lag, last + 1):
+        for item in y_group(step):
+            y_relay(item)
+
+    @pl.when(is_root)
+    def _():
+        for item in y_order:
+            take, put = keep(item)
+            take.wait()
+            put.start()
+        for item in y_order:
+            keep(item)[1].wait()
+            each_way(y_copies(item, True), lambda copy: copy.wait_send())
+
+    @pl.when(is_relay)
+    def _():
+        for item in y_order:
+            each_way(y_copies(item, False), lambda copy: copy.wait_send())
+
+    @pl.when(jnp.logical_not(on_line))
+    def _():
+        for item in y_order:
+            y_copies(item, False)[2].wait_recv()
+
+    @pl.when(is_lead)
+    def _():
+        for k in range(1, prow):
+            for copy in lead(k):
+                copy.wait_send()
+
+    for chunk in (0, 1, 2):
+        for k in range(1, nx):
+            x_copy(chunk, k).wait_send()
+        for way in (0, 1):
+            for step in range(1, last + 1):
+                if has(way, step, chunk):
+                    z_send_copy(way, step, chunk).wait_send()
+
+
 def shards(embeddings, noise_var):
     row_count, col_count = lax.axis_size("prow"), lax.axis_size("pcol")
-    col_index = lax.axis_index("pcol")
-    local = jnp.transpose(embeddings[:, 0], (0, 2, 1))
-    rows = lax.all_gather(local, "pcol", axis=1, tiled=True)
-    row_tiles, feats, tile = rows.shape
-    col_tiles = row_tiles * row_count // col_count
+    nx, nz, ny = 4, col_count // 4, row_count // 2
+    row_tiles, _, tile, width = embeddings.shape
     ratio = col_count // row_count
-    first, first_noise = from_root(rows[0], "prow", 0), from_root(noise_var[0, 0], "prow", 0)
-    chosen = lax.dynamic_index_in_dim(
-        rows.reshape(col_tiles, ratio, feats, tile), col_index // row_count, 1, keepdims=False
+    col_tiles = row_tiles // ratio
+    local = jnp.transpose(embeddings[:, 0], (0, 2, 1)).reshape(col_tiles, ratio, width, tile)
+    noise = jnp.broadcast_to(noise_var[0].astype(F32), (8, tile))
+    pieces = 2 * nz
+    anywhere = pl.BlockSpec(memory_space=pl.ANY)
+    vmem = pl.BlockSpec(memory_space=pltpu.VMEM)
+    dma = pltpu.SemaphoreType.DMA
+    rows, cols, first, first_noise = pl.pallas_call(
+        functools.partial(gather_kernel, (nx, nz, ny)),
+        in_specs=[vmem, vmem],
+        out_specs=[anywhere, anywhere, anywhere, vmem],
+        out_shape=[
+            jax.ShapeDtypeStruct((col_tiles, ratio, nz, nx, width, tile), BF16),
+            jax.ShapeDtypeStruct((col_tiles, nz, nx, width, tile), BF16),
+            jax.ShapeDtypeStruct((nz, nx, width, tile), BF16),
+            jax.ShapeDtypeStruct((8, tile), F32),
+        ],
+        scratch_shapes=[
+            pltpu.VMEM((col_tiles, nz, nx, width, tile), BF16),
+            dma((3,)),
+            dma((2, row_count - 1)),
+            dma((2,)),
+            dma((3, nx - 1)),
+            dma((3, nx - 1)),
+            dma((2, nz // 2, 3)),
+            dma((2, nz // 2, 3)),
+            dma((pieces, 3)),
+            dma((pieces,)),
+            dma((2, pieces)),
+        ],
+        compiler_params=pltpu.CompilerParams(collective_id=0, has_side_effects=True),
+        name="gather",
+    )(local, noise)
+    feats = width * col_count
+    return finish(
+        rows.reshape(row_tiles, feats, tile),
+        cols.reshape(col_tiles, feats, tile),
+        first.reshape(feats, tile),
+        noise_var,
+        first_noise[0],
     )
-    cols = from_root(chosen, "prow", col_index % row_count)
-    return finish(rows, cols, first, noise_var, first_noise)
 
 
 def finish(rows, cols, first, noise_var, first_noise):

time: 254 us -> 106 us (0.42)
  the two profiles are of different devices: /device:TPU:1 before, /device:TPU:33 now
where the time goes in v2:
time: 106 us
  Pallas kernels  102 us (96%)
  other arithmetic  1.97 us (2%)
  local copies, waits for them, and re-layouts  1.28 us (1%)
    pallas_call x1, Pallas kernels, shards(): pl.pallas_call(functools.partial(gather_kernel, (nx, nz, ny)), in_specs=[...  74.5 us
    pallas_call x1, Pallas kernels, finish(): pl.pallas_call(factor_kernel, out_shape=jax.ShapeDtypeStruct((tile, tile)...  14.1 us
    pallas_call x1, Pallas kernels, finish(): pl.pallas_call(functools.partial(schur_kernel, row_count, col_count), gri...  13.2 us

profile of v2, /device:TPU:33, one launch (start us, length us, event | category | flops | bytes accessed | tf_op | source)
XLA Modules:
  0.0 105.6 jit_solution(6302400140480030622)
XLA Ops:
  0.6 0.7 bitcast_convert_fusion.1
  1.3 0.6 broadcast_in_dim.2.noise
  1.9 0.7 bitcast_convert_fusion
  2.6 74.5 %gather.1 = (bf16[6,2,8,4,24,128]{5,4,3,2,1,0:T(8,128)(2,1)}, bf16[6,8,4,24,128]{4,3,2,1,0:T(8,128)(2,1)}, bf16[8,4,24,128]{3,2,1,0:T(8,128)(2,1)}, f32[8,128]{1,0:T(8,128)}) custom-call(bf16[6,2,24,128]{3,2,1,0:T(8,128)(2,1)} %bitcast.22, f32[8,128]{1,0:T(8,128)} %broadcast_in_dim.2.noise), custom_call_target="tpu_custom_call" | custom-call | tf_op jit(solution)/shard_map/gather/pallas_call | solution.py:390
  77.1 0.7 slice.7.noise_ref
  77.8 0.0 copy-start
  77.8 0.6 pad_maximum_fusion.noise_ref
  78.4 0.0 copy-done
  78.4 14.1 %factor.1.inverse_ref = f32[128,128]{1,0:T(8,128)} custom-call(bf16[768,128]{1,0:T(8,128)(2,1)} %bitcast.20, f32[1,128]{1,0:T(1,128)} %copy-done), custom_call_target="tpu_custom_call" | custom-call | tf_op jit(solution)/shard_map/factor/pallas_call | solution.py:431
  92.5 13.2 %schur.1 = (f32[9216,128]{1,0:T(8,128)}, f32[48,128]{1,0:T(8,128)}) custom-call(bf16[12,768,128]{2,1,0:T(8,128)(2,1)} %bitcast.18, bf16[6,768,128]{2,1,0:T(8,128)(2,1)} %bitcast.19, bf16[768,128]{1,0:T(8,128)(2,1)} %bitcast.21, f32[13,128]{1,0:T(8,128)} %pad_maximum_fusion.noise_ref, f32[128,128]{1,0:T(8,128)} %factor.1.inverse_ref), custom_call_target="tpu_custom_call" | custom-call | tf_op jit(solution)/shard_map/schur/pallas_call | solution.py:440
Async XLA Ops:
  77.8 0.6 copy-start

commit v3 on v2

--- a/solution.py
+++ b/solution.py
@@ -79,12 +79,14 @@
 
 
 def factor_kernel(first_ref, noise_ref, inverse_ref, work):
-    inverse_ref[...] = inverse_factor(first_ref[...], noise_ref[...], work)
+    inverse_ref[...] = inverse_factor(
+        first_ref[...], noise_ref[...].astype(F32)[:1], work
+    )
 
 
 def schur_kernel(
-    row_count, col_count, row_ref, col_ref, first_ref, noise_ref, inverse_ref,
-    schur_ref, share_ref, wide, col_sq, col_panel, panel,
+    row_count, col_count, row_ref, col_ref, first_ref, noise_ref, first_noise_ref, inverse_ref,
+    schur_ref, share_ref, wide, col_sq, col_panel, panel, noise_held,
 ):
     step = pl.program_id(0)
     group, feats, tile = row_ref.shape
@@ -94,48 +96,49 @@
     diagonal = eye_mask(tile)
     first = first_ref[...]
     first_sq = feature_squares(first)
-    inverse = inverse_ref[...]
-
-    def panel_of(samples, sq, noise, is_first):
+    first_noise = jnp.where(diagonal, first_noise_ref[...].astype(F32)[:1], 0.0)
+
+    def panel_of(samples, sq, leads):
         gram = jnp.exp((2.0 * matmul(samples, first) - (sq + first_sq)) * scale)
-        gram = gram + jnp.where(diagonal & is_first, noise, 0.0)
-        return matmul_nt(gram, inverse, lax.Precision.HIGHEST)
+        head = gram[:tile] + jnp.where(leads, first_noise, 0.0)
+        gram = jnp.concatenate([head, gram[tile:]], axis=0)
+        return matmul_nt(gram, inverse_ref[...], lax.Precision.HIGHEST)
 
     @pl.when(step == 0)
     def _():
+        noise_held[...] = noise_ref[...].astype(F32)
+        samples, squares = [], []
         for d in range(col_tiles):
             block = col_ref[d]
             place = slice(d * tile, (d + 1) * tile)
             wide[:, place] = block
             sq = feature_squares(block)
             col_sq[:, place] = sq
-            noise = noise_ref[noise_ref.shape[0] - 1 :, :]
-            is_first = (q == 0) if d == 0 else False
-            col_panel[place, :] = split3(
-                panel_of(jnp.transpose(block), down(sq), noise, is_first), False
-            )
-
-    stride = col_tiles
+            samples.append(jnp.transpose(block))
+            squares.append(down(sq))
+        whole = panel_of(jnp.concatenate(samples), jnp.concatenate(squares), q == 0)
+        col_panel[...] = split3(whole, False)
+
+    samples = jnp.concatenate([jnp.transpose(row_ref[t]) for t in range(group)])
+    sq = jnp.concatenate([down(feature_squares(row_ref[t])) for t in range(group)])
+    rows = panel_of(samples, sq, step * group * row_count + r == 0)
+    panel[...] = rows
+    dots = matmul(samples, wide[...])
+    update = matmul_nt(split3(rows, True), col_panel[...])
+    tiles = [step * group + t for t in range(group)]
+    noises = [jnp.where(diagonal, noise_held[pl.ds(a, 1), :], 0.0) for a in tiles]
+    for d in range(col_tiles):
+        place = slice(d * tile, (d + 1) * tile)
+        gram = jnp.exp((2.0 * dots[:, place] - (sq + col_sq[:, place])) * scale)
+        added = jnp.concatenate([
+            jnp.where(a * row_count + r == d * col_count + q, noise, 0.0)
+            for a, noise in zip(tiles, noises)
+        ])
+        schur_ref[pl.ds(d, group * tile, stride=col_tiles), :] = gram + added - update[:, place]
     share = tile // col_count
-    shares = []
-    for t in range(group):
-        a = step * group + t
-        block = row_ref[t]
-        samples = jnp.transpose(block)
-        sq = down(feature_squares(block))
-        noise = noise_ref[pl.ds(a, 1), :]
-        rows = panel_of(samples, sq, noise, a * row_count + r == 0)
-        panel[t * tile : (t + 1) * tile, :] = rows
-        dots = matmul(samples, wide[...])
-        update = matmul_nt(split3(rows, True), col_panel[...])
-        for d in range(col_tiles):
-            place = slice(d * tile, (d + 1) * tile)
-            gram = jnp.exp((2.0 * dots[:, place] - (sq + col_sq[:, place])) * scale)
-            same = a * row_count + r == d * col_count + q
-            gram = gram + jnp.where(diagonal & same, noise, 0.0)
-            schur_ref[pl.ds(t * tile * stride + d, tile, stride=stride), :] = gram - update[:, place]
-        shares.append(panel[pl.ds(t * tile + q * share, share), :])
-    share_ref[...] = jnp.concatenate(shares, axis=0)
+    share_ref[...] = jnp.concatenate(
+        [panel[pl.ds(t * tile + q * share, share), :] for t in range(group)]
+    )
 
 
 def gather_kernel(
@@ -157,6 +160,7 @@
     is_relay = on_line & (place != 0)
     is_lead = r == 0
     far = ny // 2
+    away = jnp.minimum(place, ny - place)
     goes_up = place < far
     goes_down = (place == 0) | (place > far + 1)
 
@@ -307,12 +311,23 @@
             each_way(y_copies(item, True), lambda copy: copy.start())
             keep(item)[0].start()
 
-    def y_relay(item):
-        @pl.when(is_relay)
-        def _():
-            copies = y_copies(item, False)
-            copies[2].wait_recv()
-            each_way(copies, lambda copy: copy.start())
+    lags = range(1, far)
+
+    def y_relay(step):
+        for lag in lags:
+            later = step <= last
+            groups = [step - lag] if later else range(max(last + 1 - lag, 0), last + 1)
+            groups = [group for group in groups if group >= 0]
+            if not groups:
+                continue
+
+            @pl.when(is_relay & ((away == lag) if lag != far - 1 else (away >= lag)))
+            def _(groups=groups):
+                for group in groups:
+                    for item in y_group(group):
+                        copies = y_copies(item, False)
+                        copies[2].wait_recv()
+                        each_way(copies, lambda copy: copy.start())
 
     for chunk in (0, 1, 2):
         if chunk == 1:
@@ -323,7 +338,6 @@
             z_send_copy(way, 1, chunk).start()
         if chunk:
             y_start((0, 0, chunk - 1))
-    lag = 2
     for step in range(2, last + 2):
         for chunk in (0, 1, 2):
             for way in (0, 1):
@@ -333,12 +347,8 @@
                         z_send_copy(way, step, chunk).start()
                     if chunk:
                         y_start((step - 1, way, chunk - 1))
-        if step - 1 >= lag:
-            for item in y_group(step - 1 - lag):
-                y_relay(item)
-    for step in range(last + 1 - lag, last + 1):
-        for item in y_group(step):
-            y_relay(item)
+        y_relay(step - 1)
+    y_relay(last + 1)
 
     @pl.when(is_root)
     def _():
@@ -382,7 +392,6 @@
     ratio = col_count // row_count
     col_tiles = row_tiles // ratio
     local = jnp.transpose(embeddings[:, 0], (0, 2, 1)).reshape(col_tiles, ratio, width, tile)
-    noise = jnp.broadcast_to(noise_var[0].astype(F32), (8, tile))
     pieces = 2 * nz
     anywhere = pl.BlockSpec(memory_space=pl.ANY)
     vmem = pl.BlockSpec(memory_space=pltpu.VMEM)
@@ -395,7 +404,7 @@
             jax.ShapeDtypeStruct((col_tiles, ratio, nz, nx, width, tile), BF16),
             jax.ShapeDtypeStruct((col_tiles, nz, nx, width, tile), BF16),
             jax.ShapeDtypeStruct((nz, nx, width, tile), BF16),
-            jax.ShapeDtypeStruct((8, tile), F32),
+            jax.ShapeDtypeStruct((row_tiles, tile), BF16),
         ],
         scratch_shapes=[
             pltpu.VMEM((col_tiles, nz, nx, width, tile), BF16),
@@ -412,14 +421,14 @@
         ],
         compiler_params=pltpu.CompilerParams(collective_id=0, has_side_effects=True),
         name="gather",
-    )(local, noise)
+    )(local, noise_var[:, 0])
     feats = width * col_count
     return finish(
         rows.reshape(row_tiles, feats, tile),
         cols.reshape(col_tiles, feats, tile),
         first.reshape(feats, tile),
         noise_var,
-        first_noise[0],
+        first_noise,
     )
 
 
@@ -427,13 +436,13 @@
     row_count, col_count = lax.axis_size("prow"), lax.axis_size("pcol")
     row_tiles, feats, tile = rows.shape
     col_tiles = cols.shape[0]
-    noise = jnp.concatenate([noise_var[:, 0], first_noise[None]], axis=0).astype(F32)
+    noise = noise_var[:, 0]
     inverse = pl.pallas_call(
         factor_kernel,
         out_shape=jax.ShapeDtypeStruct((tile, tile), F32),
         scratch_shapes=[pltpu.VMEM((tile, tile), F32)],
         name="factor",
-    )(first, noise[row_tiles:])
+    )(first, first_noise)
     group = 2
     share = tile // col_count
     height = group * tile * col_tiles
@@ -444,7 +453,8 @@
             pl.BlockSpec((group, feats, tile), lambda i: (i, 0, 0)),
             pl.BlockSpec((col_tiles, feats, tile), lambda i: (0, 0, 0)),
             pl.BlockSpec((feats, tile), lambda i: (0, 0)),
-            pl.BlockSpec((row_tiles + 1, tile), lambda i: (0, 0)),
+            pl.BlockSpec((row_tiles, tile), lambda i: (0, 0)),
+            pl.BlockSpec((row_tiles, tile), lambda i: (0, 0)),
             pl.BlockSpec((tile, tile), lambda i: (0, 0)),
         ],
         out_specs=[
@@ -460,9 +470,10 @@
             pltpu.VMEM((1, col_tiles * tile), F32),
             pltpu.VMEM((col_tiles * tile, 3 * tile), BF16),
             pltpu.VMEM((group * tile, tile), F32),
+            pltpu.VMEM((row_tiles, tile), F32),
         ],
         name="schur",
-    )(rows, cols, first, noise, inverse)
+    )(rows, cols, first, noise, first_noise, inverse)
     return (
         schur.reshape(row_tiles, 1, tile, col_tiles, 1, tile),
         shared.reshape(row_tiles, 1, share, tile),

time: 106 us -> 94 us (0.89)
  the two profiles are of different devices: /device:TPU:33 before, /device:TPU:129 now
where the time goes in v3:
time: 94 us; the launch traced here: 93.6 us
  Pallas kernels  93 us (99%)
    pallas_call x1, Pallas kernels, shards(): pl.pallas_call(functools.partial(gather_kernel, (nx, nz, ny)), in_specs=[...  67.5 us
    pallas_call x1, Pallas kernels, finish(): pl.pallas_call(factor_kernel, out_shape=jax.ShapeDtypeStruct((tile, tile)...  14 us
    pallas_call x1, Pallas kernels, finish(): pl.pallas_call(functools.partial(schur_kernel, row_count, col_count), gri...  11.4 us

profile of v3, /device:TPU:129, one launch (start us, length us, event | category | flops | bytes accessed | tf_op | source)
XLA Modules:
  0.0 93.6 jit_solution(4866122225297771531)
XLA Ops:
  0.6 67.5 %gather.1 = (bf16[6,2,8,4,24,128]{5,4,3,2,1,0:T(8,128)(2,1)}, bf16[6,8,4,24,128]{4,3,2,1,0:T(8,128)(2,1)}, bf16[8,4,24,128]{3,2,1,0:T(8,128)(2,1)}, bf16[12,128]{1,0:T(8,128)(2,1)}) custom-call(bf16[6,2,24,128]{3,2,1,0:T(8,128)(2,1)} %bitcast.17, bf16[12,128]{1,0:T(8,128)(2,1)} %bitcast.18), custom_call_target="tpu_custom_call" | custom-call | tf_op jit(solution)/shard_map/gather/pallas_call | solution.py:399
  68.2 14.0 %factor.1.inverse_ref = f32[128,128]{1,0:T(8,128)} custom-call(bf16[768,128]{1,0:T(8,128)(2,1)} %bitcast.15, bf16[12,128]{1,0:T(8,128)(2,1)} %get-tuple-element.11.noise_ref.first_noise_ref), custom_call_target="tpu_custom_call" | custom-call | tf_op jit(solution)/shard_map/factor/pallas_call | solution.py:440
  82.2 11.4 %schur.1 = (f32[9216,128]{1,0:T(8,128)}, f32[48,128]{1,0:T(8,128)}) custom-call(bf16[12,768,128]{2,1,0:T(8,128)(2,1)} %bitcast.13, bf16[6,768,128]{2,1,0:T(8,128)(2,1)} %bitcast.14, bf16[768,128]{1,0:T(8,128)(2,1)} %bitcast.16, bf16[12,128]{1,0:T(8,128)(2,1)} %bitcast.19, bf16[12,128]{1,0:T(8,128)(2,1)} %get-tuple-element.11.noise_ref.first_noise_ref, ...), custom_call_target="tpu_custom_call" | custom-call | tf_op jit(solution)/shard_map/schur/pallas_call | solution.py:449

commit v4 on v3

--- a/solution.py
+++ b/solution.py
@@ -43,45 +43,50 @@
     )
 
 
-def inverse_factor(first, noise, work):
-    feats, tile = first.shape
+PIECES = 8
+
+
+def start_factor(first, noise, work):
+    feats = first.shape[0]
     sq = feature_squares(first)
     dots = matmul(jnp.transpose(first), first)
     gram = jnp.exp((2.0 * dots - (down(sq) + sq)) * (1.0 / feats))
+    work[...] = gram + jnp.where(eye_mask(first.shape[1]), noise, 0.0)
+
+
+def eliminate(work, piece):
+    tile = work.shape[1]
+    part = tile // PIECES
+    base = piece * part
+    height = tile - base
+    lanes = lax.broadcasted_iota(jnp.int32, (height, tile), 1)
+    ids = lax.broadcasted_iota(jnp.int32, (height, tile), 0) + base
+
+    def step(k, carry):
+        held = work[base:, :]
+        at_k = lanes == k
+        pivot = work[pl.ds(k, 1), :]
+        here = at_k[:1]
+        inv = 1.0 / jnp.sum(jnp.where(here, pivot, 0.0), axis=1, keepdims=True)
+        column = jnp.sum(jnp.where(at_k, held, 0.0), axis=1, keepdims=True)
+        scaled = jnp.where(here, 1.0, pivot) * inv
+        factor = jnp.where(ids > k, column, 0.0)
+        cleared = jnp.where(at_k & (ids > k), 0.0, held)
+        work[base:, :] = cleared - factor * scaled
+        return carry
+
+    lax.fori_loop(base, base + part, step, 0)
+
+
+def end_factor(work):
+    tile = work.shape[1]
     diagonal = eye_mask(tile)
-    work[...] = gram + jnp.where(diagonal, noise, 0.0)
-    part = tile // 4
-    for base in range(0, tile, part):
-        height = tile - base
-        lanes = lax.broadcasted_iota(jnp.int32, (height, tile), 1)
-        ids = lax.broadcasted_iota(jnp.int32, (height, tile), 0) + base
-
-        def step(k, carry, base=base, lanes=lanes, ids=ids):
-            held = work[base:, :]
-            at_k = lanes == k
-            pivot = work[pl.ds(k, 1), :]
-            here = at_k[:1]
-            inv = 1.0 / jnp.sum(jnp.where(here, pivot, 0.0), axis=1, keepdims=True)
-            column = jnp.sum(jnp.where(at_k, held, 0.0), axis=1, keepdims=True)
-            scaled = jnp.where(here, 1.0, pivot) * inv
-            factor = jnp.where(ids > k, column, 0.0)
-            cleared = jnp.where(at_k & (ids > k), 0.0, held)
-            work[base:, :] = cleared - factor * scaled
-            return carry
-
-        lax.fori_loop(base, base + part, step, 0)
     done = work[...]
     pivots = jnp.sum(jnp.where(diagonal, done, 0.0), axis=1, keepdims=True)
     rows = lax.broadcasted_iota(jnp.int32, (tile, tile), 0)
     cols = lax.broadcasted_iota(jnp.int32, (tile, tile), 1)
     unit = jnp.where(cols < rows, done, jnp.where(diagonal, 1.0, 0.0))
     return unit * (1.0 / jnp.sqrt(pivots))
-
-
-def factor_kernel(first_ref, noise_ref, inverse_ref, work):
-    inverse_ref[...] = inverse_factor(
-        first_ref[...], noise_ref[...].astype(F32)[:1], work
-    )
 
 
 def schur_kernel(
@@ -142,8 +147,8 @@
 
 
 def gather_kernel(
-    shape, local, noise, rows, cols, first, first_noise,
-    held, own_sem, lead_send, lead_recv, x_send, x_recv, z_send, z_recv, y_send, y_recv, root_sem,
+    shape, local, noise, rows, cols, first, first_noise, inverse,
+    held, first_held, work, own_sem, lead_send, lead_recv, x_send, x_recv, z_send, z_recv, y_send, y_recv, root_sem,
 ):
     nx, nz, ny = shape
     col_tiles, ratio = rows.shape[:2]
@@ -329,6 +334,15 @@
                         copies[2].wait_recv()
                         each_way(copies, lambda copy: copy.start())
 
+    def z_pass(step, chunk):
+        for way in (0, 1):
+            if has(way, step, chunk):
+                z_arrived(way, step, chunk)
+                if step < last and has(way, step + 1, chunk):
+                    z_send_copy(way, step + 1, chunk).start()
+                if chunk:
+                    y_start((step, way, chunk - 1))
+
     for chunk in (0, 1, 2):
         if chunk == 1:
             own.wait()
@@ -338,17 +352,31 @@
             z_send_copy(way, 1, chunk).start()
         if chunk:
             y_start((0, 0, chunk - 1))
-    for step in range(2, last + 2):
-        for chunk in (0, 1, 2):
-            for way in (0, 1):
-                if has(way, step - 1, chunk):
-                    z_arrived(way, step - 1, chunk)
-                    if step <= last and has(way, step, chunk):
-                        z_send_copy(way, step, chunk).start()
-                    if chunk:
-                        y_start((step - 1, way, chunk - 1))
-        y_relay(step - 1)
+
+    fetch = pltpu.make_async_copy(first, first_held, own_sem.at[3])
+    jobs = [functools.partial(eliminate, work, piece) for piece in range(PIECES)]
+    ahead = 1
+    for step in range(1, last + 1):
+        for chunk in (1, 2):
+            if ahead <= last:
+                z_pass(ahead, 0)
+                if ahead == last:
+                    fetch.start()
+            elif ahead == last + 1:
+                fetch.wait()
+                leading = first_held[...].astype(F32).reshape(-1, first.shape[-1]).astype(BF16)
+                start_factor(leading, first_noise[...].astype(F32)[:1], work)
+            else:
+                jobs.pop(0)()
+            ahead += 1
+            z_pass(step, chunk)
+        y_relay(step)
+    for job in jobs[:2]:
+        job()
     y_relay(last + 1)
+    for job in jobs[2:]:
+        job()
+    inverse[...] = end_factor(work)
 
     @pl.when(is_root)
     def _():
@@ -396,19 +424,22 @@
     anywhere = pl.BlockSpec(memory_space=pl.ANY)
     vmem = pl.BlockSpec(memory_space=pltpu.VMEM)
     dma = pltpu.SemaphoreType.DMA
-    rows, cols, first, first_noise = pl.pallas_call(
+    rows, cols, first, first_noise, inverse = pl.pallas_call(
         functools.partial(gather_kernel, (nx, nz, ny)),
         in_specs=[vmem, vmem],
-        out_specs=[anywhere, anywhere, anywhere, vmem],
+        out_specs=[anywhere, anywhere, anywhere, vmem, vmem],
         out_shape=[
             jax.ShapeDtypeStruct((col_tiles, ratio, nz, nx, width, tile), BF16),
             jax.ShapeDtypeStruct((col_tiles, nz, nx, width, tile), BF16),
             jax.ShapeDtypeStruct((nz, nx, width, tile), BF16),
             jax.ShapeDtypeStruct((row_tiles, tile), BF16),
+            jax.ShapeDtypeStruct((tile, tile), F32),
         ],
         scratch_shapes=[
             pltpu.VMEM((col_tiles, nz, nx, width, tile), BF16),
-            dma((3,)),
+            pltpu.VMEM((nz, nx, width, tile), BF16),
+            pltpu.VMEM((tile, tile), F32),
+            dma((4,)),
             dma((2, row_count - 1)),
             dma((2,)),
             dma((3, nx - 1)),
@@ -429,20 +460,15 @@
         first.reshape(feats, tile),
         noise_var,
         first_noise,
+        inverse,
     )
 
 
-def finish(rows, cols, first, noise_var, first_noise):
+def finish(rows, cols, first, noise_var, first_noise, inverse):
     row_count, col_count = lax.axis_size("prow"), lax.axis_size("pcol")
     row_tiles, feats, tile = rows.shape
     col_tiles = cols.shape[0]
     noise = noise_var[:, 0]
-    inverse = pl.pallas_call(
-        factor_kernel,
-        out_shape=jax.ShapeDtypeStruct((tile, tile), F32),
-        scratch_shapes=[pltpu.VMEM((tile, tile), F32)],
-        name="factor",
-    )(first, first_noise)
     group = 2
     share = tile // col_count
     height = group * tile * col_tiles

time: 94 us -> 85.1 us (0.905)
  the two profiles are of different devices: /device:TPU:129 before, /device:TPU:128 now
where the time goes in v4:
time: 85.1 us; the launch traced here: 84.7 us
  Pallas kernels  84.1 us (99%)
    pallas_call x1, Pallas kernels, shards(): pl.pallas_call(functools.partial(gather_kernel, (nx, nz, ny)), in_specs=[...  72.7 us
    pallas_call x1, Pallas kernels, finish(): pl.pallas_call(functools.partial(schur_kernel, row_count, col_count), gri...  11.4 us

profile of v4, /device:TPU:128, one launch (start us, length us, event | category | flops | bytes accessed | tf_op | source)
XLA Modules:
  0.0 84.7 jit_solution(18341475274576343374)
XLA Ops:
  0.6 72.7 %gather.1 = (bf16[6,2,8,4,24,128]{5,4,3,2,1,0:T(8,128)(2,1)}, bf16[6,8,4,24,128]{4,3,2,1,0:T(8,128)(2,1)}, bf16[8,4,24,128]{3,2,1,0:T(8,128)(2,1)}, bf16[12,128]{1,0:T(8,128)(2,1)}, f32[128,128]{1,0:T(8,128)}) custom-call(bf16[6,2,24,128]{3,2,1,0:T(8,128)(2,1)} %bitcast.16, bf16[12,128]{1,0:T(8,128)(2,1)} %bitcast.17), custom_call_target="tpu_custom_call" | custom-call | tf_op jit(solution)/shard_map/gather/pallas_call | solution.py:427
  73.3 11.4 %schur.1 = (f32[9216,128]{1,0:T(8,128)}, f32[48,128]{1,0:T(8,128)}) custom-call(bf16[12,768,128]{2,1,0:T(8,128)(2,1)} %bitcast.13, bf16[6,768,128]{2,1,0:T(8,128)(2,1)} %bitcast.14, bf16[768,128]{1,0:T(8,128)(2,1)} %bitcast.15, bf16[12,128]{1,0:T(8,128)(2,1)} %bitcast.18, bf16[12,128]{1,0:T(8,128)(2,1)} %get-tuple-element.12.first_noise_ref, ...), custom_call_target="tpu_custom_call" | custom-call | tf_op jit(solution)/shard_map/schur/pallas_call | solution.py:475

commit v5 on v4

--- a/solution.py
+++ b/solution.py
@@ -316,23 +316,30 @@
             each_way(y_copies(item, True), lambda copy: copy.start())
             keep(item)[0].start()
 
+    def event_of(item):
+        step, _, piece = item
+        return 2 * (step - 1) + piece
+
     lags = range(1, far)
-
-    def y_relay(step):
+    events = 2 * last
+
+    def y_relay(now):
         for lag in lags:
-            later = step <= last
-            groups = [step - lag] if later else range(max(last + 1 - lag, 0), last + 1)
-            groups = [group for group in groups if group >= 0]
-            if not groups:
+            if now < events:
+                items = [item for item in y_order if event_of(item) == now - lag]
+                if now == 0:
+                    items = [item for item in y_order if event_of(item) <= -lag]
+            else:
+                items = [item for item in y_order if event_of(item) >= events - lag]
+            if not items:
                 continue
 
             @pl.when(is_relay & ((away == lag) if lag != far - 1 else (away >= lag)))
-            def _(groups=groups):
-                for group in groups:
-                    for item in y_group(group):
-                        copies = y_copies(item, False)
-                        copies[2].wait_recv()
-                        each_way(copies, lambda copy: copy.start())
+            def _(items=items):
+                for item in items:
+                    copies = y_copies(item, False)
+                    copies[2].wait_recv()
+                    each_way(copies, lambda copy: copy.start())
 
     def z_pass(step, chunk):
         for way in (0, 1):
@@ -346,6 +353,8 @@
     for chunk in (0, 1, 2):
         if chunk == 1:
             own.wait()
+        if chunk == 2:
+            z_pass(1, 0)
         for k in range(1, nx):
             x_copy(chunk, k).wait_recv()
         for way in (0, 1):
@@ -354,28 +363,32 @@
             y_start((0, 0, chunk - 1))
 
     fetch = pltpu.make_async_copy(first, first_held, own_sem.at[3])
-    jobs = [functools.partial(eliminate, work, piece) for piece in range(PIECES)]
-    ahead = 1
-    for step in range(1, last + 1):
-        for chunk in (1, 2):
-            if ahead <= last:
-                z_pass(ahead, 0)
-                if ahead == last:
-                    fetch.start()
-            elif ahead == last + 1:
-                fetch.wait()
-                leading = first_held[...].astype(F32).reshape(-1, first.shape[-1]).astype(BF16)
-                start_factor(leading, first_noise[...].astype(F32)[:1], work)
-            else:
-                jobs.pop(0)()
-            ahead += 1
-            z_pass(step, chunk)
-        y_relay(step)
-    for job in jobs[:2]:
-        job()
-    y_relay(last + 1)
-    for job in jobs[2:]:
-        job()
+    done = 0
+    for now in range(events):
+        step, chunk = now // 2 + 1, now % 2 + 1
+        if now + 2 <= last:
+            z_pass(now + 2, 0)
+            if now + 2 == last:
+                fetch.start()
+        elif now + 1 == last:
+            fetch.wait()
+            leading = first_held[...].astype(F32).reshape(-1, first.shape[-1]).astype(BF16)
+            start_factor(leading, first_noise[...].astype(F32)[:1], work)
+        else:
+            eliminate(work, done)
+            done += 1
+        z_pass(step, chunk)
+        y_relay(now)
+
+    hands_on = is_relay & (away < far)
+
+    def rest():
+        for piece in range(done, PIECES):
+            eliminate(work, piece)
+
+    pl.when(jnp.logical_not(hands_on))(rest)
+    y_relay(events)
+    pl.when(hands_on)(rest)
     inverse[...] = end_factor(work)
 
     @pl.when(is_root)

time: 85.1 us -> 84.2 us (0.989)
  the two profiles are of different devices: /device:TPU:128 before, /device:TPU:24 now
where the time goes in v5:
time: 84.2 us; the launch traced here: 83.8 us
  Pallas kernels  83.2 us (99%)
    pallas_call x1, Pallas kernels, shards(): pl.pallas_call(functools.partial(gather_kernel, (nx, nz, ny)), in_specs=[...  71.7 us
    pallas_call x1, Pallas kernels, finish(): pl.pallas_call(functools.partial(schur_kernel, row_count, col_count), gri...  11.4 us

profile of v5, /device:TPU:24, one launch (start us, length us, event | category | flops | bytes accessed | tf_op | source)
XLA Modules:
  0.0 83.8 jit_solution(6043046094088464343)
XLA Ops:
  0.6 71.7 %gather.1 = (bf16[6,2,8,4,24,128]{5,4,3,2,1,0:T(8,128)(2,1)}, bf16[6,8,4,24,128]{4,3,2,1,0:T(8,128)(2,1)}, bf16[8,4,24,128]{3,2,1,0:T(8,128)(2,1)}, bf16[12,128]{1,0:T(8,128)(2,1)}, f32[128,128]{1,0:T(8,128)}) custom-call(bf16[6,2,24,128]{3,2,1,0:T(8,128)(2,1)} %bitcast.16, bf16[12,128]{1,0:T(8,128)(2,1)} %bitcast.17), custom_call_target="tpu_custom_call" | custom-call | tf_op jit(solution)/shard_map/gather/pallas_call | solution.py:440
  72.4 11.4 %schur.1 = (f32[9216,128]{1,0:T(8,128)}, f32[48,128]{1,0:T(8,128)}) custom-call(bf16[12,768,128]{2,1,0:T(8,128)(2,1)} %bitcast.13, bf16[6,768,128]{2,1,0:T(8,128)(2,1)} %bitcast.14, bf16[768,128]{1,0:T(8,128)(2,1)} %bitcast.15, bf16[12,128]{1,0:T(8,128)(2,1)} %bitcast.18, bf16[12,128]{1,0:T(8,128)(2,1)} %get-tuple-element.12.first_noise_ref, ...), custom_call_target="tpu_custom_call" | custom-call | tf_op jit(solution)/shard_map/schur/pallas_call | solution.py:488

commit v6 on v5

--- a/solution.py
+++ b/solution.py
@@ -148,7 +148,7 @@
 
 def gather_kernel(
     shape, local, noise, rows, cols, first, first_noise, inverse,
-    held, first_held, work, own_sem, lead_send, lead_recv, x_send, x_recv, z_send, z_recv, y_send, y_recv, root_sem,
+    held, first_held, work, own_sem, lead_send, lead_recv, x_send, x_recv, z_send, z_recv, y_send, y_recv, root_sem, share_sem,
 ):
     nx, nz, ny = shape
     col_tiles, ratio = rows.shape[:2]
@@ -363,33 +363,36 @@
             y_start((0, 0, chunk - 1))
 
     fetch = pltpu.make_async_copy(first, first_held, own_sem.at[3])
+    off_line = jnp.logical_not(on_line)
+
+    def begin():
+        fetch.wait()
+        leading = first_held[...].astype(F32).reshape(-1, first.shape[-1]).astype(BF16)
+        start_factor(leading, first_noise[...].astype(F32)[:1], work)
+
     done = 0
     for now in range(events):
         step, chunk = now // 2 + 1, now % 2 + 1
         if now + 2 <= last:
             z_pass(now + 2, 0)
             if now + 2 == last:
-                fetch.start()
+                pl.when(off_line)(fetch.start)
         elif now + 1 == last:
-            fetch.wait()
-            leading = first_held[...].astype(F32).reshape(-1, first.shape[-1]).astype(BF16)
-            start_factor(leading, first_noise[...].astype(F32)[:1], work)
+            pl.when(off_line)(begin)
         else:
-            eliminate(work, done)
+            pl.when(off_line)(functools.partial(eliminate, work, done))
             done += 1
         z_pass(step, chunk)
         y_relay(now)
 
-    hands_on = is_relay & (away < far)
-
-    def rest():
+    @pl.when(off_line)
+    def _():
         for piece in range(done, PIECES):
             eliminate(work, piece)
-
-    pl.when(jnp.logical_not(hands_on))(rest)
+        inverse[...] = end_factor(work)
+
     y_relay(events)
-    pl.when(hands_on)(rest)
-    inverse[...] = end_factor(work)
+    handed = remote(inverse, inverse, share_sem.at[0], share_sem.at[1], 2 * y + 1 - core, q)
 
     @pl.when(is_root)
     def _():
@@ -406,10 +409,18 @@
         for item in y_order:
             each_way(y_copies(item, False), lambda copy: copy.wait_send())
 
-    @pl.when(jnp.logical_not(on_line))
-    def _():
+    @pl.when(off_line)
+    def _():
+        late = [item for item in y_order if event_of(item) >= events - far]
         for item in y_order:
+            if item not in late:
+                y_copies(item, False)[2].wait_recv()
+        handed.start()
+        for item in late:
             y_copies(item, False)[2].wait_recv()
+        handed.wait_send()
+
+    pl.when(on_line)(handed.wait_recv)
 
     @pl.when(is_lead)
     def _():
@@ -462,6 +473,7 @@
             dma((pieces, 3)),
             dma((pieces,)),
             dma((2, pieces)),
+            dma((2,)),
         ],
         compiler_params=pltpu.CompilerParams(collective_id=0, has_side_effects=True),
         name="gather",

time: 84.2 us -> 82.2 us (0.976)
  the two profiles are of different devices: /device:TPU:24 before, /device:TPU:33 now
where the time goes in v6:
time: 82.2 us; the launch traced here: 81.8 us
  Pallas kernels  81.2 us (99%)
    pallas_call x1, Pallas kernels, shards(): pl.pallas_call(functools.partial(gather_kernel, (nx, nz, ny)), in_specs=[...  69.7 us
    pallas_call x1, Pallas kernels, finish(): pl.pallas_call(functools.partial(schur_kernel, row_count, col_count), gri...  11.4 us

profile of v6, /device:TPU:33, one launch (start us, length us, event | category | flops | bytes accessed | tf_op | source)
XLA Modules:
  0.0 81.8 jit_solution(15421685217437403486)
XLA Ops:
  0.6 69.7 %gather.1 = (bf16[6,2,8,4,24,128]{5,4,3,2,1,0:T(8,128)(2,1)}, bf16[6,8,4,24,128]{4,3,2,1,0:T(8,128)(2,1)}, bf16[8,4,24,128]{3,2,1,0:T(8,128)(2,1)}, bf16[12,128]{1,0:T(8,128)(2,1)}, f32[128,128]{1,0:T(8,128)}) custom-call(bf16[6,2,24,128]{3,2,1,0:T(8,128)(2,1)} %bitcast.16, bf16[12,128]{1,0:T(8,128)(2,1)} %bitcast.17), custom_call_target="tpu_custom_call" | custom-call | tf_op jit(solution)/shard_map/gather/pallas_call | solution.py:451
  70.4 11.4 %schur.1 = (f32[9216,128]{1,0:T(8,128)}, f32[48,128]{1,0:T(8,128)}) custom-call(bf16[12,768,128]{2,1,0:T(8,128)(2,1)} %bitcast.13, bf16[6,768,128]{2,1,0:T(8,128)(2,1)} %bitcast.14, bf16[768,128]{1,0:T(8,128)(2,1)} %bitcast.15, bf16[12,128]{1,0:T(8,128)(2,1)} %bitcast.18, bf16[12,128]{1,0:T(8,128)(2,1)} %get-tuple-element.12.first_noise_ref, ...), custom_call_target="tpu_custom_call" | custom-call | tf_op jit(solution)/shard_map/schur/pallas_call | solution.py:500

commit v7 on v6

--- a/solution.py
+++ b/solution.py
@@ -160,9 +160,12 @@
     owner = lax.rem(q, prow)
     side = lax.div(q, prow)
     place = lax.rem(y - lax.div(owner, 2) + ny, ny)
-    on_line = core == lax.rem(owner, 2)
-    is_root = on_line & (place == 0)
-    is_relay = on_line & (place != 0)
+    main = core == lax.rem(owner, 2)
+    relay_core = 1 - lax.rem(owner, 2)
+    is_root = main & (place == 0)
+    is_relay = jnp.logical_not(main) & (place != 0)
+    is_end = jnp.logical_not(is_root | is_relay)
+    owner_ring = lax.rem(r, nx) == x
     is_lead = r == 0
     far = ny // 2
     away = jnp.minimum(place, ny - place)
@@ -179,7 +182,7 @@
         return nx * near_z(shift) + x
 
     def y_peer(shift):
-        return 2 * lax.rem(y + shift + ny, ny) + core
+        return 2 * lax.rem(y + shift + ny, ny) + relay_core
 
     def remote(src, dst, send, recv, row, col):
         return pltpu.make_async_remote_copy(
@@ -363,7 +366,7 @@
             y_start((0, 0, chunk - 1))
 
     fetch = pltpu.make_async_copy(first, first_held, own_sem.at[3])
-    off_line = jnp.logical_not(on_line)
+    early = main & jnp.logical_not(owner_ring)
 
     def begin():
         fetch.wait()
@@ -376,16 +379,22 @@
         if now + 2 <= last:
             z_pass(now + 2, 0)
             if now + 2 == last:
-                pl.when(off_line)(fetch.start)
+                pl.when(main)(fetch.start)
         elif now + 1 == last:
-            pl.when(off_line)(begin)
+            pl.when(early)(begin)
         else:
-            pl.when(off_line)(functools.partial(eliminate, work, done))
+            pl.when(early)(functools.partial(eliminate, work, done))
             done += 1
         z_pass(step, chunk)
         y_relay(now)
 
-    @pl.when(off_line)
+    @pl.when(main & owner_ring)
+    def _():
+        begin()
+        for piece in range(done):
+            eliminate(work, piece)
+
+    @pl.when(main)
     def _():
         for piece in range(done, PIECES):
             eliminate(work, piece)
@@ -409,18 +418,23 @@
         for item in y_order:
             each_way(y_copies(item, False), lambda copy: copy.wait_send())
 
-    @pl.when(off_line)
-    def _():
-        late = [item for item in y_order if event_of(item) >= events - far]
+    late = [item for item in y_order if event_of(item) >= events - far]
+
+    @pl.when(is_end)
+    def _():
         for item in y_order:
             if item not in late:
                 y_copies(item, False)[2].wait_recv()
-        handed.start()
+
+    pl.when(main)(handed.start)
+
+    @pl.when(is_end)
+    def _():
         for item in late:
             y_copies(item, False)[2].wait_recv()
-        handed.wait_send()
-
-    pl.when(on_line)(handed.wait_recv)
+
+    pl.when(main)(handed.wait_send)
+    pl.when(jnp.logical_not(main))(handed.wait_recv)
 
     @pl.when(is_lead)
     def _():

time: 82.2 us -> 81.7 us (level)
  the two profiles are of different devices: /device:TPU:33 before, /device:TPU:1 now
where the time goes in v7:
time: 81.7 us; the launch traced here: 81.3 us
  Pallas kernels  80.7 us (99%)
    pallas_call x1, Pallas kernels, shards(): pl.pallas_call(functools.partial(gather_kernel, (nx, nz, ny)), in_specs=[...  69.3 us
    pallas_call x1, Pallas kernels, finish(): pl.pallas_call(functools.partial(schur_kernel, row_count, col_count), gri...  11.4 us

profile of v7, /device:TPU:1, one launch (start us, length us, event | category | flops | bytes accessed | tf_op | source)
XLA Modules:
  0.0 81.3 jit_solution(4507385932820622646)
XLA Ops:
  0.6 69.3 %gather.1 = (bf16[6,2,8,4,24,128]{5,4,3,2,1,0:T(8,128)(2,1)}, bf16[6,8,4,24,128]{4,3,2,1,0:T(8,128)(2,1)}, bf16[8,4,24,128]{3,2,1,0:T(8,128)(2,1)}, bf16[12,128]{1,0:T(8,128)(2,1)}, f32[128,128]{1,0:T(8,128)}) custom-call(bf16[6,2,24,128]{3,2,1,0:T(8,128)(2,1)} %bitcast.16, bf16[12,128]{1,0:T(8,128)(2,1)} %bitcast.17), custom_call_target="tpu_custom_call" | custom-call | tf_op jit(solution)/shard_map/gather/pallas_call | solution.py:465
  69.9 11.4 %schur.1 = (f32[9216,128]{1,0:T(8,128)}, f32[48,128]{1,0:T(8,128)}) custom-call(bf16[12,768,128]{2,1,0:T(8,128)(2,1)} %bitcast.13, bf16[6,768,128]{2,1,0:T(8,128)(2,1)} %bitcast.14, bf16[768,128]{1,0:T(8,128)(2,1)} %bitcast.15, bf16[12,128]{1,0:T(8,128)(2,1)} %bitcast.18, bf16[12,128]{1,0:T(8,128)(2,1)} %get-tuple-element.12.first_noise_ref, ...), custom_call_target="tpu_custom_call" | custom-call | tf_op jit(solution)/shard_map/schur/pallas_call | solution.py:514

commit v8 on v7

--- a/solution.py
+++ b/solution.py
@@ -165,7 +165,6 @@
     is_root = main & (place == 0)
     is_relay = jnp.logical_not(main) & (place != 0)
     is_end = jnp.logical_not(is_root | is_relay)
-    owner_ring = lax.rem(r, nx) == x
     is_lead = r == 0
     far = ny // 2
     away = jnp.minimum(place, ny - place)
@@ -366,7 +365,6 @@
             y_start((0, 0, chunk - 1))
 
     fetch = pltpu.make_async_copy(first, first_held, own_sem.at[3])
-    early = main & jnp.logical_not(owner_ring)
 
     def begin():
         fetch.wait()
@@ -381,18 +379,12 @@
             if now + 2 == last:
                 pl.when(main)(fetch.start)
         elif now + 1 == last:
-            pl.when(early)(begin)
+            pl.when(main)(begin)
         else:
-            pl.when(early)(functools.partial(eliminate, work, done))
+            pl.when(main)(functools.partial(eliminate, work, done))
             done += 1
         z_pass(step, chunk)
         y_relay(now)
-
-    @pl.when(main & owner_ring)
-    def _():
-        begin()
-        for piece in range(done):
-            eliminate(work, piece)
 
     @pl.when(main)
     def _():

time: 81.7 us -> 78.1 us (0.956)
  the two profiles are of different devices: /device:TPU:1 before, /device:TPU:129 now
where the time goes in v8:
time: 78.1 us; the launch traced here: 77.7 us
  Pallas kernels  77.1 us (99%)
    pallas_call x1, Pallas kernels, shards(): pl.pallas_call(functools.partial(gather_kernel, (nx, nz, ny)), in_specs=[...  65.7 us
    pallas_call x1, Pallas kernels, finish(): pl.pallas_call(functools.partial(schur_kernel, row_count, col_count), gri...  11.4 us

profile of v8, /device:TPU:129, one launch (start us, length us, event | category | flops | bytes accessed | tf_op | source)
XLA Modules:
  0.0 77.7 jit_solution(15585161431918585933)
XLA Ops:
  0.6 65.7 %gather.1 = (bf16[6,2,8,4,24,128]{5,4,3,2,1,0:T(8,128)(2,1)}, bf16[6,8,4,24,128]{4,3,2,1,0:T(8,128)(2,1)}, bf16[8,4,24,128]{3,2,1,0:T(8,128)(2,1)}, bf16[12,128]{1,0:T(8,128)(2,1)}, f32[128,128]{1,0:T(8,128)}) custom-call(bf16[6,2,24,128]{3,2,1,0:T(8,128)(2,1)} %bitcast.16, bf16[12,128]{1,0:T(8,128)(2,1)} %bitcast.17), custom_call_target="tpu_custom_call" | custom-call | tf_op jit(solution)/shard_map/gather/pallas_call | solution.py:457
  66.3 11.4 %schur.1 = (f32[9216,128]{1,0:T(8,128)}, f32[48,128]{1,0:T(8,128)}) custom-call(bf16[12,768,128]{2,1,0:T(8,128)(2,1)} %bitcast.13, bf16[6,768,128]{2,1,0:T(8,128)(2,1)} %bitcast.14, bf16[768,128]{1,0:T(8,128)(2,1)} %bitcast.15, bf16[12,128]{1,0:T(8,128)(2,1)} %bitcast.18, bf16[12,128]{1,0:T(8,128)(2,1)} %get-tuple-element.12.first_noise_ref, ...), custom_call_target="tpu_custom_call" | custom-call | tf_op jit(solution)/shard_map/schur/pallas_call | solution.py:506
